TPU v7x, 256 devices: a whole 4x4x8 slice. The times are simulated.
256 devices in a mesh: leaf: 64 (over z, y, core), panel: 4 (over x).
Axes of the slice: x: 4, y: 4, z: 8, core: 2. Of those that a mesh axis runs over, the one named last changes fastest.
Arguments:
- right_sides: float32 [7, 4096, 512], P(None, 'leaf', 'panel'), may hold values from -11 to 11
- inverse_diagonal: bfloat16 [7, 4096, 4096], P(None, 'leaf'), may hold values from -1 to 2, as said below
- off_diagonal: bfloat16 [6, 4096, 4096], P(None, 'leaf'), may hold values from -0.0625 to 0.0625
- structure: int32 [6, 32], replicated, may hold values from 0 to 95, as said below
- pivot_counts: int32 [7], replicated, may hold values from 2048 to 4096, as said below
Outputs:
- samples: float32 [7, 4096, 512], P(None, 'leaf', 'panel')
- sample_power: float32 [7, 4096], P(None, 'leaf')
Inputs may be any that keep to these rules, and one draw needn't show every extreme that they name: `inverse_diagonal`: zero below the diagonal; diagonal entries positive. `structure`: a front of the middle level lists 4096 // 128 distinct blocks of the root (numbers below 32); a bottom front lists distinct blocks of the root and of its parent (parent p = 1 + (f - 3) // 2 holds block numbers p * 32 to (p + 1) * 32 - 1). `pivot_counts`: rows from the count on are padding; some front has exactly 4096 live rows and some exactly 2048.
All inputs are finite; a program needn't handle non-finite values.
Results may differ from a plain program's by a relative error of at most 0.0038.
Values may be sent and summed in bfloat16 or wider, within the bound.
No kernel may reach another device: no remote copies, remote signals or barrier semaphores. Data moves between devices by JAX's collectives and lax.ppermute only.
A program may use at most 64 MiB of HBM per device.

v0:
```python
import jax
import jax.numpy as jnp
from jax import lax
from jax.sharding import PartitionSpec as P


def share_rows(stored_rows):
    return lax.all_gather(stored_rows, "leaf", axis=1, tiled=True)


def solve_fronts(rhs_block, update, inverse, live_mask):
    reduced = (live_mask * (rhs_block - update)).astype(jnp.bfloat16)
    running = jnp.einsum(
        "fij,fjr->fir",
        inverse,
        lax.all_gather(reduced, "leaf", axis=1, tiled=True),
        preferred_element_type=jnp.float32,
    )
    return live_mask * running


def couple(blocks, picked):
    return jnp.einsum("fik,fkr->fir", blocks, picked, preferred_element_type=jnp.float32)


def local(right_sides, inverse_diagonal, off_diagonal, structure, pivot_counts):
    rows_local = right_sides.shape[1]
    columns_dev = right_sides.shape[2]
    pivot_rows = inverse_diagonal.shape[2]
    coupled = off_diagonal.shape[2]
    block_size = coupled // structure.shape[1]
    first_row = lax.axis_index("leaf") * rows_local
    position = first_row + jnp.arange(rows_local, dtype=jnp.int32)
    live_rows = (position[None, :] < pivot_counts[:, None]).astype(jnp.float32)[:, :, None]
    wanted = (
        structure[:, :, None] * block_size + jnp.arange(block_size, dtype=jnp.int32)[None, None, :]
    ).reshape(6, coupled)
    pieces = 1
    block_width = columns_dev // pieces
    root_solved = solve_fronts(
        right_sides[0:1], jnp.zeros_like(right_sides[0:1]), inverse_diagonal[0:1], live_rows[0:1]
    )
    root_all = share_rows(root_solved.astype(jnp.bfloat16))[0]
    middle_update = couple(off_diagonal[0:2], jnp.take(root_all, wanted[0:2], axis=0))
    middle = solve_fronts(right_sides[1:3], middle_update, inverse_diagonal[1:3], live_rows[1:3])
    middle_all = share_rows(middle.astype(jnp.bfloat16)).reshape(2 * pivot_rows, block_width)
    ancestors = jnp.concatenate([root_all, middle_all], axis=0)
    bottom_update = couple(off_diagonal[2:6], jnp.take(ancestors, wanted[2:6], axis=0))
    bottom = solve_fronts(right_sides[3:7], bottom_update, inverse_diagonal[3:7], live_rows[3:7])
    results = jnp.concatenate([root_solved, middle, bottom], axis=0)
    squares = lax.psum(jnp.sum(results * results, axis=2), "panel")
    sample_power = squares / jnp.float32(columns_dev * lax.axis_size("panel"))
    return (results, sample_power)


def solution(mesh):
    placed = (P(None, "leaf", "panel"), P(None, "leaf", None), P(None, "leaf", None), P(), P())
    return jax.shard_map(
        local,
        mesh=mesh,
        in_specs=placed,
        out_specs=(P(None, "leaf", "panel"), P(None, "leaf")),
        check_vma=False,
    )
```

profile of v0, /device:TPU:1, one launch (start us, length us, event | category | flops | bytes accessed | tf_op | source)
XLA Modules:
  0.0 513.6 jit_solution(4271180809915617018)
XLA Ops:
  7.2 0.0 all-gather.7.cloned.1.call-start
  7.2 0.7 compare_convert_fusion
  8.0 1.4 multiply_convert_fusion
  9.4 0.0 all-gather.7.cloned.1.call-update
  9.4 0.0 all-gather.15.cloned.1.call-start
  9.5 82.9 %all-gather.7.cloned.1.call-done = bf16[1,4096,128]{2,1,0:T(8,128)(2,1)} async-done(((bf16[1,64,128]{2,1,0:T(8,128)(2,1)}), bf16[1,4096,128]{2,1,0:T(8,128)(2,1)}) %all-gather.7.cloned.1.call-update) | async-done | bytes 1048592 | tf_op jit(solution)/shard_map/all_gather | solution.py:16
  92.3 2.3 bitcast_convert_fusion
  94.7 0.0 all-gather.15.cloned.1.call-update
  94.7 0.0 all-gather.9.cloned.1.call-start
  94.7 0.7 broadcast_multiply_fusion.1
  95.4 0.1 iota_add_fusion
  95.6 0.1 compare_and_fusion.1
  95.7 74.6 %all-gather.15.cloned.1.call-done = bf16[4096,128]{1,0:T(8,128)(2,1)} async-done(((bf16[64,128]{1,0:T(8,128)(2,1)}), bf16[4096,128]{1,0:T(8,128)(2,1)}) %all-gather.15.cloned.1.call-update) | async-done | bytes 1048592 | tf_op jit(solution)/shard_map/all_gather | solution.py:8
  170.3 23.2 %gather_fusion = bf16[8192,128]{1,0:T(8,128)(2,1)S(1)} fusion(bf16[4096,128]{1,0:T(8,128)(2,1)} %all-gather.15.cloned.1.call-done, s32[8192]{0:T(1024)S(1)} %broadcast_clamp_fusion.1), kind=kCustom, calls=%fused_computation | custom fusion | bytes 4227072 | tf_op jit(solution)/shard_map/jit(_take)/gather | solution.py:44
  193.5 3.3 fusion.46
  196.8 0.0 all-gather.9.cloned.1.call-update
  196.8 0.0 all-gather.11.cloned.1.call-start
  196.9 75.4 %all-gather.9.cloned.1.call-done = bf16[2,4096,128]{2,1,0:T(8,128)(2,1)} async-done(((bf16[2,64,128]{2,1,0:T(8,128)(2,1)}), bf16[2,4096,128]{2,1,0:T(8,128)(2,1)}) %all-gather.9.cloned.1.call-update) | async-done | bytes 2097168 | tf_op jit(solution)/shard_map/all_gather | solution.py:16
  272.3 3.0 fusion.59
  275.3 0.0 all-gather.11.cloned.1.call-update
  275.3 0.0 all-gather.13.cloned.1.call-start
  275.5 0.1 compare_and_fusion
  275.6 74.9 %all-gather.11.cloned.1.call-done = bf16[2,4096,128]{2,1,0:T(8,128)(2,1)} async-done(((bf16[2,64,128]{2,1,0:T(8,128)(2,1)}), bf16[2,4096,128]{2,1,0:T(8,128)(2,1)}) %all-gather.11.cloned.1.call-update) | async-done | bytes 2097168 | tf_op jit(solution)/shard_map/all_gather | solution.py:8
  350.5 2.8 pad_maximum_fusion
  353.3 57.8 %gather_fusion.1 = bf16[16384,128]{1,0:T(8,128)(2,1)} fusion(bf16[12288,128]{1,0:T(8,128)(2,1)S(1)} %pad_maximum_fusion, s32[16384]{0:T(1024)S(1)} %broadcast_clamp_fusion), kind=kCustom, calls=%fused_computation.1 | custom fusion | bytes 8454144 | tf_op jit(solution)/shard_map/jit(_take)/gather | solution.py:48
  411.1 5.9 %fusion.31 = bf16[4,64,128]{2,1,0:T(8,128)(2,1)} fusion(bf16[4,4096,128]{2,1,0:T(8,128)(2,1)} %bitcast.59, pred[4,4096]{1,0:T(4,128)(4,1)S(1)} %compare_and_fusion, bf16[6,64,4096]{2,1,0:T(8,128)(2,1)} %param.7, f32[7,64,128]{2,1,0:T(8,128)} %param.5, f32[4,64]{1,0:T(4,128)S(1)} %slice.62), kind=kOutput, calls=%fused_computation.18 | convolution fusion | flops 270630912 | bytes 6505472 | tf_op jit(solution)/shard_map/fik,fkr->fir/dot_general | solution.py:23
  417.1 0.0 all-gather.13.cloned.1.call-update
  417.1 76.6 %all-gather.13.cloned.1.call-done = bf16[4,4096,128]{2,1,0:T(8,128)(2,1)} async-done(((bf16[4,64,128]{2,1,0:T(8,128)(2,1)}), bf16[4,4096,128]{2,1,0:T(8,128)(2,1)}) %all-gather.13.cloned.1.call-update) | async-done | bytes 4194320 | tf_op jit(solution)/shard_map/all_gather | solution.py:16
  493.7 3.7 fusion.13
  497.4 0.7 multiply_reduce_fusion
  498.1 8.4 %psum.7 = f32[7,64]{1,0:T(8,128)S(1)} all-reduce(f32[7,64]{1,0:T(8,128)S(1)} %get-tuple-element.2), channel_id=1, replica_groups=mesh['leaf'=64,'panel'=4] {'panel'}, use_global_device_ids=true, to_apply=%region_1.2 | all-reduce | flops 448 | bytes 3584 | tf_op jit(solution)/shard_map/psum | solution.py:51
  506.4 0.6 broadcast_multiply_fusion
  (14 shorter events, 0.2 us)
Async XLA Ops:
  7.2 85.2 %all-gather.7.cloned.1.call-start = ((), (), s32[]{:S(2)}) async-start(), calls=%async_computation | async-start | bytes 1064960 | tf_op jit(solution)/shard_map/all_gather | solution.py:16
  9.4 160.8 %all-gather.15.cloned.1.call-start = ((), (), s32[]{:S(2)}) async-start(), calls=%async_computation.4 | async-start | bytes 1064960 | tf_op jit(solution)/shard_map/all_gather | solution.py:8
  94.7 177.6 %all-gather.9.cloned.1.call-start = ((), (), s32[]{:S(2)}) async-start(), calls=%async_computation.1 | async-start | bytes 2129920 | tf_op jit(solution)/shard_map/all_gather | solution.py:16
  196.8 153.7 %all-gather.11.cloned.1.call-start = ((), (), s32[]{:S(2)}) async-start(), calls=%async_computation.2 | async-start | bytes 2129920 | tf_op jit(solution)/shard_map/all_gather | solution.py:8
  275.3 218.4 %all-gather.13.cloned.1.call-start = ((), (), s32[]{:S(2)}) async-start(), calls=%async_computation.3 | async-start | bytes 4259840 | tf_op jit(solution)/shard_map/all_gather | solution.py:16
Sparse Core Ops, SparseCore 0:
  11.3 80.9 all-gather.6
  95.7 74.5 all-gather.14
  196.9 75.2 all-gather.8
  275.5 74.9 all-gather.10
  417.2 76.4 all-gather.12
where the time goes:
time: 514 us
  waiting for transfers between devices  384 us (75%)
  local copies, waits for them, and re-layouts  81.1 us (16%)
  matrix products  18.3 us (4%)
  between operations  13.9 us (3%)
  blocking collectives  8.37 us (2%)
  other arithmetic  7.24 us (1%)
    all_gather x3, waiting for transfers between devices, solve_fronts(): lax.all_gather(reduced, 'leaf', axis=1, tiled=True)  235 us
    all_gather x2, waiting for transfers between devices, share_rows(): return lax.all_gather(stored_rows, 'leaf', axis=1, tiled=True)  149 us
    gather x1, local copies, waits for them, and re-layouts, local(): jnp.take(ancestors, wanted[2:6], axis=0)  57.8 us
    gather x1, local copies, waits for them, and re-layouts, local(): jnp.take(root_all, wanted[0:2], axis=0)  23.2 us
  transfers between devices with their start and end apart: 5, of which 5 were waited for; matrix products, arithmetic and copies ran while one was open for 0% of the time, Pallas kernels for 0%

commit v1 on v0

--- a/solution.py
+++ b/solution.py
@@ -5,7 +5,9 @@
 
 
 def share_rows(stored_rows):
-    return lax.all_gather(stored_rows, "leaf", axis=1, tiled=True)
+    return jnp.concatenate(
+        lax.all_to_all(jnp.stack([stored_rows] * lax.axis_size("leaf")), "leaf", 0, 0), axis=1
+    )
 
 
 def solve_fronts(rhs_block, update, inverse, live_mask):

time: 514 us -> 460 us (0.89)
  waiting for transfers between devices: 384 us -> 312 us
  starting transfers between devices: 0.21 us -> 13.2 us
    all_gather x2 -> x0, waiting for transfers between devices: 149 us -> none  [share_rows(): return lax.all_gather(stored_rows, 'leaf', axis=1, tiled=True)]
    all_to_all x0 -> x2, waiting for transfers between devices: none -> 77.3 us  [share_rows(): lax.all_to_all(jnp.stack([stored_rows] * lax.axis_size('leaf')), 'leaf',...]
    all_to_all x0 -> x2, starting transfers between devices: none -> 13.1 us  [share_rows(): lax.all_to_all(jnp.stack([stored_rows] * lax.axis_size('leaf')), 'leaf',...]
where the time goes in v1:
time: 460 us; the launch traced here: 459 us
  waiting for transfers between devices  312 us (68%)
  local copies, waits for them, and re-layouts  85.2 us (19%)
  matrix products  17 us (4%)
  between operations  14 us (3%)
  starting transfers between devices  13.2 us (3%)
  other arithmetic  9.07 us (2%)
  blocking collectives  8.37 us (2%)
    all_gather x3, waiting for transfers between devices, solve_fronts(): lax.all_gather(reduced, 'leaf', axis=1, tiled=True)  235 us
    all_to_all x2, waiting for transfers between devices, share_rows(): lax.all_to_all(jnp.stack([stored_rows] * lax.axis_size('leaf')), 'leaf',...  77.3 us
    gather x1, local copies, waits for them, and re-layouts, local(): jnp.take(ancestors, wanted[2:6], axis=0)  57.8 us
    gather x1, local copies, waits for them, and re-layouts, local(): jnp.take(root_all, wanted[0:2], axis=0)  24 us
    all_to_all x2, starting transfers between devices, share_rows(): lax.all_to_all(jnp.stack([stored_rows] * lax.axis_size('leaf')), 'leaf',...  13.1 us
    dot_general x2, matrix products, couple(): jnp.einsum('fik,fkr->fir', blocks, picked, preferred_element_type=jnp.flo...  9.26 us
  transfers between devices with their start and end apart: 5, of which 5 were waited for; matrix products, arithmetic and copies ran while one was open for 0% of the time, Pallas kernels for 0%

profile of v1, /device:TPU:1, one launch (start us, length us, event | category | flops | bytes accessed | tf_op | source)
XLA Modules:
  0.0 459.3 jit_solution(2346195720533651646)
XLA Ops:
  7.2 0.0 all-gather.4.cloned.1.call-start
  7.2 0.7 compare_convert_fusion
  8.0 1.4 multiply_convert_fusion
  9.4 0.0 all-gather.4.cloned.1.call-update
  9.4 82.9 %all-gather.4.cloned.1.call-done = bf16[1,4096,128]{2,1,0:T(8,128)(2,1)} async-done(((bf16[1,64,128]{2,1,0:T(8,128)(2,1)}), bf16[1,4096,128]{2,1,0:T(8,128)(2,1)}) %all-gather.4.cloned.1.call-update) | async-done | bytes 1048592 | tf_op jit(solution)/shard_map/all_gather | solution.py:18
  92.4 1.7 bitcast_convert_fusion
  94.1 1.2 stack.4
  95.3 6.7 %all-to-all-start = ((bf16[64,1,64,128]{3,2,1,0:T(8,128)(2,1)}), bf16[64,1,64,128]{3,2,1,0:T(8,128)(2,1)S(1)}, u32[]{:S(2)}, u32[]{:S(2)}) async-start(bf16[64,1,64,128]{3,2,1,0:T(8,128)(2,1)} %stack.4), calls=%async_computation | async-start | bytes 2097152 | tf_op jit(solution)/shard_map/all_to_all | solution.py:9
  102.0 0.0 all-gather.6.cloned.1.call-start
  102.1 0.1 iota_add_fusion
  102.3 0.1 compare_and_fusion.1
  102.4 27.8 %all-to-all-done = bf16[64,1,64,128]{3,2,1,0:T(8,128)(2,1)S(1)} async-done(((bf16[64,1,64,128]{3,2,1,0:T(8,128)(2,1)}), bf16[64,1,64,128]{3,2,1,0:T(8,128)(2,1)S(1)}, u32[]{:S(2)}, u32[]{:S(2)}) %all-to-all-start) | async-done | bytes 1048608 | tf_op jit(solution)/shard_map/all_to_all | solution.py:9
  130.2 24.0 %gather_fusion = bf16[8192,128]{1,0:T(8,128)(2,1)S(1)} fusion(bf16[4096,128]{1,0:T(8,128)(2,1)S(1)} %bitcast.61, s32[8192]{0:T(1024)S(1)} %broadcast_clamp_fusion.1), kind=kCustom, calls=%fused_computation | custom fusion | bytes 4227072 | tf_op jit(solution)/shard_map/jit(_take)/gather | solution.py:46
  154.3 3.3 fusion.46
  157.6 0.0 all-gather.6.cloned.1.call-update
  157.6 75.0 %all-gather.6.cloned.1.call-done = bf16[2,4096,128]{2,1,0:T(8,128)(2,1)} async-done(((bf16[2,64,128]{2,1,0:T(8,128)(2,1)}), bf16[2,4096,128]{2,1,0:T(8,128)(2,1)}) %all-gather.6.cloned.1.call-update) | async-done | bytes 2097168 | tf_op jit(solution)/shard_map/all_gather | solution.py:18
  232.6 2.4 fusion.59
  235.0 1.9 stack.5
  236.9 6.4 %all-to-all-start.1 = ((bf16[64,2,64,128]{3,2,1,0:T(8,128)(2,1)}), bf16[64,2,64,128]{3,2,1,0:T(8,128)(2,1)S(1)}, u32[]{:S(2)}, u32[]{:S(2)}) async-start(bf16[64,2,64,128]{3,2,1,0:T(8,128)(2,1)} %stack.5), calls=%async_computation.1 | async-start | bytes 4194304 | tf_op jit(solution)/shard_map/all_to_all | solution.py:9
  243.3 0.0 all-gather.8.cloned.1.call-start
  243.4 0.1 compare_and_fusion
  243.5 49.5 %all-to-all-done.1 = bf16[64,2,64,128]{3,2,1,0:T(8,128)(2,1)S(1)} async-done(((bf16[64,2,64,128]{3,2,1,0:T(8,128)(2,1)}), bf16[64,2,64,128]{3,2,1,0:T(8,128)(2,1)S(1)}, u32[]{:S(2)}, u32[]{:S(2)}) %all-to-all-start.1) | async-done | bytes 2097184 | tf_op jit(solution)/shard_map/all_to_all | solution.py:9
  293.0 0.2 copy.7
  293.1 5.3 %pad_maximum_fusion = bf16[12288,128]{1,0:T(8,128)(2,1)S(1)} fusion(bf16[8192,128]{1,0:T(8,128)(2,1)S(1)} %bitcast.63, bf16[4096,128]{1,0:T(8,128)(2,1)} %bitcast.62), kind=kLoop, calls=%fused_computation.5 | loop fusion | flops 6291456 | bytes 6291456 | tf_op jit(solution)/shard_map/concatenate | solution.py:49
  298.5 57.8 %gather_fusion.1 = bf16[16384,128]{1,0:T(8,128)(2,1)} fusion(bf16[12288,128]{1,0:T(8,128)(2,1)S(1)} %pad_maximum_fusion, s32[16384]{0:T(1024)S(1)} %broadcast_clamp_fusion), kind=kCustom, calls=%fused_computation.1 | custom fusion | bytes 8454144 | tf_op jit(solution)/shard_map/jit(_take)/gather | solution.py:50
  356.3 5.9 %fusion.31 = bf16[4,64,128]{2,1,0:T(8,128)(2,1)} fusion(bf16[4,4096,128]{2,1,0:T(8,128)(2,1)} %bitcast.65, pred[4,4096]{1,0:T(4,128)(4,1)S(1)} %compare_and_fusion, bf16[6,64,4096]{2,1,0:T(8,128)(2,1)} %param.7, f32[7,64,128]{2,1,0:T(8,128)} %param.5, f32[4,64]{1,0:T(4,128)S(1)} %slice.62), kind=kOutput, calls=%fused_computation.18 | convolution fusion | flops 270630912 | bytes 6505472 | tf_op jit(solution)/shard_map/fik,fkr->fir/dot_general | solution.py:25
  362.2 0.0 all-gather.8.cloned.1.call-update
  362.3 77.2 %all-gather.8.cloned.1.call-done = bf16[4,4096,128]{2,1,0:T(8,128)(2,1)} async-done(((bf16[4,64,128]{2,1,0:T(8,128)(2,1)}), bf16[4,4096,128]{2,1,0:T(8,128)(2,1)}) %all-gather.8.cloned.1.call-update) | async-done | bytes 4194320 | tf_op jit(solution)/shard_map/all_gather | solution.py:18
  439.5 3.7 fusion.13
  443.1 0.7 multiply_reduce_fusion
  443.8 8.4 %psum.7 = f32[7,64]{1,0:T(8,128)S(1)} all-reduce(f32[7,64]{1,0:T(8,128)S(1)} %get-tuple-element.2), channel_id=1, replica_groups=mesh['leaf'=64,'panel'=4] {'panel'}, use_global_device_ids=true, to_apply=%region_1.2 | all-reduce | flops 448 | bytes 3584 | tf_op jit(solution)/shard_map/psum | solution.py:53
  452.2 0.6 broadcast_multiply_fusion
  (19 shorter events, 0.2 us)
Async XLA Ops:
  7.2 94.9 %copy-start.1 = (s32[6,32]{1,0:T(8,128)S(1)}, s32[6,32]{1,0:T(8,128)}, u32[]{:S(2)}) copy-start(s32[6,32]{1,0:T(8,128)} %param.8) | copy-start | bytes 2308
  7.2 85.2 %all-gather.4.cloned.1.call-start = ((), (), s32[]{:S(2)}) async-start(), calls=%async_computation.2 | async-start | bytes 1064960 | tf_op jit(solution)/shard_map/all_gather | solution.py:18
  95.3 34.9 %all-to-all-start = ((bf16[64,1,64,128]{3,2,1,0:T(8,128)(2,1)}), bf16[64,1,64,128]{3,2,1,0:T(8,128)(2,1)S(1)}, u32[]{:S(2)}, u32[]{:S(2)}) async-start(bf16[64,1,64,128]{3,2,1,0:T(8,128)(2,1)} %stack.4), calls=%async_computation | async-start | bytes 2097152 | tf_op jit(solution)/shard_map/all_to_all | solution.py:9
  102.0 130.6 %all-gather.6.cloned.1.call-start = ((), (), s32[]{:S(2)}) async-start(), calls=%async_computation.3 | async-start | bytes 2129920 | tf_op jit(solution)/shard_map/all_gather | solution.py:18
  130.2 24.0 %copy-start = (bf16[64,1,64,128]{3,2,1,0:T(8,128)(2,1)}, bf16[64,1,64,128]{3,2,1,0:T(8,128)(2,1)S(1)}, u32[]{:S(2)}) copy-start(bf16[64,1,64,128]{3,2,1,0:T(8,128)(2,1)S(1)} %all-to-all-done) | copy-start | bytes 3145732
  236.9 56.1 %all-to-all-start.1 = ((bf16[64,2,64,128]{3,2,1,0:T(8,128)(2,1)}), bf16[64,2,64,128]{3,2,1,0:T(8,128)(2,1)S(1)}, u32[]{:S(2)}, u32[]{:S(2)}) async-start(bf16[64,2,64,128]{3,2,1,0:T(8,128)(2,1)} %stack.5), calls=%async_computation.1 | async-start | bytes 4194304 | tf_op jit(solution)/shard_map/all_to_all | solution.py:9
  243.3 196.2 %all-gather.8.cloned.1.call-start = ((), (), s32[]{:S(2)}) async-start(), calls=%async_computation.4 | async-start | bytes 4259840 | tf_op jit(solution)/shard_map/all_gather | solution.py:18
Sparse Core Ops, SparseCore 0:
  11.3 80.9 all-gather.3
  157.7 74.8 all-gather.5
  362.4 77.0 all-gather.7
